TPU v7x, 512 devices: a whole 4x4x16 slice. The times are simulated.
512 devices in a mesh: seq: 128 (over x, y, z_lo), dp: 4 (over z_hi, core).
Axes of the slice: x: 4, y: 4, z: 16 (z_hi: 2, z_lo: 8; z = z_hi * 8 + z_lo), core: 2. Of those that a mesh axis runs over, the one named last changes fastest.
Arguments:
- bases: int32 [4, 16384], P('dp', 'seq'), may hold values from 0 to 3
- lengths: int32 [4, 128], P('dp', 'seq'), may hold values from 64 to 128, as said below
- cotangent: bfloat16 [4, 16384, 768], P('dp', 'seq'), may hold values from -6 to 6
- first_conv_taps: bfloat16 [3, 768, 384], P(None, 'seq'), may hold values from -0.125 to 0.125
- first_projection: bfloat16 [384, 768], P('seq'), may hold values from -0.3125 to 0.3125
- second_conv_taps: bfloat16 [3, 768, 384], P(None, 'seq'), may hold values from -0.125 to 0.125
- second_projection: bfloat16 [384, 768], P('seq'), may hold values from -0.3125 to 0.3125
- embed: float32 [4, 768], replicated, may hold values from -6 to 6
Outputs:
- saliency: float32 [4, 4, 16384], P('dp', None, 'seq')
- grad_proj: float32 [589824], P(('seq', 'dp'))
Inputs may be any that keep to these rules, and one draw needn't show every extreme that they name: `lengths`: every block holds between 64 and 128 live rows; in each window one block holds exactly 128 and another exactly 64.
All inputs are finite; a program needn't handle non-finite values.
Results may differ from a plain program's by a relative error of at most 0.0042.
Values may be sent and summed in bfloat16 or wider, within the bound.
A program may use at most 64 MiB of HBM per device.

v0:
```python
import math

import jax
import jax.numpy as jnp
from jax import lax
from jax.sharding import PartitionSpec as P

FIRST_DILATION = 16
SECOND_DILATION = 64


SQRT_HALF = 0.7071067811865476
INV_SQRT_TWO_PI = 0.3989422804014327


def extended_2(block, sides, width):
    for axis, dim in sides:
        count = lax.axis_size(axis)
        forward = [(i, i + 1) for i in range(count - 1)]
        backward = [(target, source) for source, target in forward]
        low = lax.ppermute(
            lax.slice_in_dim(block, block.shape[dim] - width, None, axis=dim), axis, forward
        )
        high = lax.ppermute(lax.slice_in_dim(block, 0, width, axis=dim), axis, backward)
        block = jnp.concatenate([low, block, high], axis=dim)
    return block


def from_partner(array, axis, bit):
    return lax.ppermute(array, axis, [(i, i ^ 1 << bit) for i in range(lax.axis_size(axis))])


def gelu_value(values):
    return 0.5 * values * (1.0 + lax.erf(values * SQRT_HALF))


def gelu_slope(values):
    return (
        0.5 * (1.0 + lax.erf(values * SQRT_HALF))
        + values * jnp.exp(-0.5 * values * values) * INV_SQRT_TWO_PI
    )


def flip_live(values, live_count, axis_idx):
    return jnp.roll(jnp.flip(values, axis_idx), live_count - values.shape[axis_idx], axis=axis_idx)


def fetch(conv_shard, proj_shard):
    return (
        lax.all_gather(conv_shard, "seq", axis=1, tiled=True),
        lax.all_gather(proj_shard, "seq", axis=0, tiled=True),
    )


def widen(values, counts, dilation):
    head_rows = values[:, :dilation]
    tail_rows = jnp.stack(
        [
            lax.dynamic_slice_in_dim(values[member], counts[member] - dilation, dilation, 0)
            for member in range(2)
        ]
    )
    rim_rows = jnp.concatenate([head_rows, tail_rows], axis=1)
    padded = extended_2(rim_rows, (("seq", 1),), dilation)
    left_rim = padded[:, :dilation]
    right_rim = padded[:, 3 * dilation :]
    zero_rows = jnp.zeros((2, dilation, values.shape[2]), values.dtype)
    extended = jnp.concatenate([left_rim, values, zero_rows], axis=1)
    return jnp.stack(
        [
            lax.dynamic_update_slice_in_dim(
                extended[member], right_rim[member], counts[member] + dilation, 0
            )
            for member in range(2)
        ]
    )


def taps_forward(extended, weights, dilation, capacity, tap_order):
    results = []
    for member in range(2):
        summed = jnp.zeros((capacity, weights.shape[2]), jnp.float32)
        for offset in range(3):
            window_rows = extended[member, offset * dilation : offset * dilation + capacity]
            summed = summed + jnp.dot(
                window_rows, weights[tap_order[member][offset]], preferred_element_type=jnp.float32
            )
        results.append(summed)
    return jnp.stack(results)


def taps_backward(extended, weights, dilation, capacity, tap_order):
    results = []
    for member in range(2):
        summed = jnp.zeros((capacity, weights.shape[1]), jnp.float32)
        for offset in range(3):
            window_rows = extended[member, offset * dilation : offset * dilation + capacity]
            weight_idx = tap_order[member][2 - offset]
            summed = summed + lax.dot_general(
                window_rows,
                weights[weight_idx],
                (((1,), (1,)), ((), ())),
                preferred_element_type=jnp.float32,
            )
        results.append(summed)
    return jnp.stack(results)


def shards(
    bases,
    lengths,
    cotangent,
    first_conv_taps,
    first_projection,
    second_conv_taps,
    second_projection,
    embed,
):
    capacity = bases.shape[1]
    channels = embed.shape[1]
    own_count = lengths[0, 0]
    own_bases = bases[0]
    own_cot = cotangent[0]
    positions = jnp.arange(capacity, dtype=jnp.int32)
    own_live = positions < own_count
    mirror_bits = lax.axis_size("seq").bit_length() - 1
    flipped_cot = jnp.where(
        own_live[:, None], flip_live(own_cot, own_count, 0), jnp.zeros_like(own_cot)
    )
    flipped_codes = (3 - flip_live(own_bases, own_count, 0)).astype(jnp.bfloat16)
    partner_info = jnp.stack(
        [
            jnp.where(own_live, flipped_codes, jnp.zeros_like(flipped_codes)),
            own_live.astype(jnp.bfloat16),
        ]
    )
    for bit_index in range(mirror_bits):
        flipped_cot, partner_info = from_partner((flipped_cot, partner_info), "seq", bit_index)
    other_count = jnp.sum(partner_info[1].astype(jnp.float32)).astype(jnp.int32)
    other_bases = partner_info[0].astype(jnp.int32)
    tap_order = ((0, 1, 2), (0, 1, 2))
    counts = jnp.stack([own_count, other_count])
    live = (positions[None, :] < counts[:, None]).astype(jnp.float32)[:, :, None]
    codes = jnp.stack([own_bases, other_bases])
    stream = jnp.zeros((2, capacity, channels), jnp.float32)
    for code_value in range(4):
        stream = stream + jnp.where(
            (codes == code_value)[:, :, None], embed[code_value][None, None, :], 0.0
        )
    stream = stream * live
    cot_half = 0.5 * jnp.stack([own_cot, flipped_cot]).astype(jnp.float32) * live
    residual_blocks = [
        (first_conv_taps, first_projection, FIRST_DILATION),
        (second_conv_taps, second_projection, SECOND_DILATION),
    ]
    kept = []
    saved = []
    for conv_shard, proj_shard, dilation in residual_blocks:
        conv_full, proj_full = fetch(conv_shard, proj_shard)
        kept.append((conv_full, proj_full))
        active = gelu_value(stream).astype(jnp.bfloat16)
        extended = widen(active, counts, dilation)
        before = taps_forward(extended, conv_full, dilation, capacity, tap_order) * live
        middle = gelu_value(before).astype(jnp.bfloat16)
        saved.append((stream, before, middle))
        stream = stream + jnp.einsum(
            "srb,bc->src", middle, proj_full, preferred_element_type=jnp.float32
        )
    grad_rows = cot_half
    proj_grads = [None, None]
    for block_idx in (1, 0):
        conv_shard, proj_shard, dilation = residual_blocks[block_idx]
        conv_full, proj_full = fetch(conv_shard, proj_shard)
        stream_in, before, middle = saved[block_idx]
        grad_low = grad_rows.astype(jnp.bfloat16)
        proj_grads[block_idx] = jnp.einsum(
            "srb,src->bc", middle, grad_low, preferred_element_type=jnp.float32
        )
        back_mid = jnp.einsum(
            "src,bc->srb", grad_low, proj_full, preferred_element_type=jnp.float32
        )
        grad_before = (back_mid * gelu_slope(before) * live).astype(jnp.bfloat16)
        extended = widen(grad_before, counts, dilation)
        grad_active = taps_backward(extended, conv_full, dilation, capacity, tap_order)
        grad_rows = grad_rows + grad_active * gelu_slope(stream_in) * live
    own_sal = jnp.einsum("bc,rc->br", embed, grad_rows[0], precision=lax.Precision.HIGHEST)
    other_sal = jnp.einsum("bc,rc->br", embed[::-1], grad_rows[1], precision=lax.Precision.HIGHEST)
    other_live = (positions < other_count).astype(jnp.float32)[None, :]
    other_sal = flip_live(other_sal, other_count, 1) * other_live
    for bit_index in range(mirror_bits):
        other_sal = from_partner(other_sal, "seq", bit_index)
    saliency = (own_sal + other_sal) * own_live.astype(jnp.float32)[None, :] / math.sqrt(channels)
    device_count = lax.axis_size("seq") * lax.axis_size("dp")
    scale = 1.0 / math.sqrt(device_count * capacity)
    terms = jnp.concatenate([proj_grads[0].reshape(-1), proj_grads[1].reshape(-1)]) * scale
    grad_part = lax.psum_scatter(terms, ("seq", "dp"), scatter_dimension=0, tiled=True)
    return (saliency[None], grad_part)


def solution(mesh):
    in_specs = (
        P("dp", "seq"),
        P("dp", "seq"),
        P("dp", "seq", None),
        P(None, "seq", None),
        P("seq", None),
        P(None, "seq", None),
        P("seq", None),
        P(),
    )
    out_specs = (P("dp", None, "seq"), P(("seq", "dp")))
    return jax.shard_map(shards, mesh=mesh, in_specs=in_specs, out_specs=out_specs, check_vma=False)
```

profile of v0, /device:TPU:6, one launch (start us, length us, event | category | flops | bytes accessed | tf_op | source)
XLA Modules:
  0.0 2492.8 jit_solution(9202959401066517145)
XLA Ops:
  10.1 3.8 collective-permute-start.7
  14.0 2.4 rev.15
  16.6 2.0 collective-permute-start
  20.0 5.2 collective-permute-start.8
  25.2 489.8 %all-gather.1 = bf16[128,3,768]{2,1,0:T(4,128)(2,1)S(1)} all-gather(bf16[1,3,768]{2,1,0:T(4,128)(2,1)} %bitcast.203), channel_id=1, replica_groups=mesh['seq'=128,'dp'=4] {'seq'}, dimensions={0}, use_global_device_ids=true | all-gather | bytes 594432 | tf_op jit(solution)/shard_map/all_gather | solution.py:51
  515.0 1.9 collective-permute-start.9
  517.0 478.8 %all-gather = bf16[128,3,768]{2,1,0:T(4,128)(2,1)S(1)} all-gather(bf16[1,3,768]{2,1,0:T(4,128)(2,1)S(1)} %bitcast.204), channel_id=1, replica_groups=mesh['seq'=128,'dp'=4] {'seq'}, dimensions={0}, use_global_device_ids=true | all-gather | bytes 594432 | tf_op jit(solution)/shard_map/all_gather | solution.py:51
  995.8 1.9 collective-permute-start.10
  1001.3 44.3 %collective-permute-start.11 = (bf16[2,128]{1,0:T(2,128)(2,1)S(1)}, bf16[2,128]{1,0:T(2,128)(2,1)S(1)}, u32[]{:S(2)}, u32[]{:S(2)}) collective-permute-start(bf16[2,128]{1,0:T(2,128)(2,1)S(1)} %collective-permute-done.10), channel_id=1, source_target_pairs={{0,64},{4,68},{8,72},{12,76},{16,80},{20,84},{24,88},{28,92},{32,9... | collective-permute-start | bytes 1544 | tf_op jit(solution)/shard_map/ppermute | solution.py:30
  1047.1 1.9 collective-permute-start.12
  1049.7 2.9 collective-permute-done.12
  1052.5 42.0 %collective-permute-start.13 = (bf16[2,128]{1,0:T(2,128)(2,1)S(1)}, bf16[2,128]{1,0:T(2,128)(2,1)S(1)}, u32[]{:S(2)}, u32[]{:S(2)}) collective-permute-start(bf16[2,128]{1,0:T(2,128)(2,1)S(1)} %collective-permute-done.12), channel_id=1, source_target_pairs={{0,256},{4,260},{8,264},{12,268},{16,272},{20,276},{24,280},{28,28... | collective-permute-start | bytes 1544 | tf_op jit(solution)/shard_map/ppermute | solution.py:30
  1098.1 1.9 collective-permute-start.1
  1100.7 8.7 collective-permute-done.1
  1109.4 1.9 collective-permute-start.2
  1111.3 1.9 collective-permute-start.14
  1113.7 13.5 collective-permute-start.15
  1127.3 2.9 collective-permute-start.3
  1130.3 4.5 collective-permute-done.3
  1134.8 1.9 collective-permute-start.4
  1136.8 7.3 collective-permute-done.4
  1144.1 3.3 collective-permute-start.5
  1148.1 3.7 collective-permute-done.5
  1151.8 5.5 collective-permute-start.6
  1157.3 6.5 fusion.61
  1168.3 1.9 collective-permute-start.16
  1170.2 705.1 %all-gather.7.cloned.1.call-done = bf16[3,768,384]{2,0,1:T(4,128)(2,1)} async-done(((bf16[3,6,384]{2,0,1:T(4,128)(2,1)}), bf16[3,768,384]{2,0,1:T(4,128)(2,1)}) %all-gather.7.cloned.1.call-update) | async-done | bytes 1769488 | tf_op jit(solution)/shard_map/all_gather | solution.py:50
  1875.3 6.6 fusion.60
  1882.0 5.5 collective-permute-start.17
  1904.3 1.9 collective-permute-start.18
  1906.2 13.8 collective-permute-start.19
  1920.0 2.4 convolution_bitcast_fusion
  1922.4 2.3 reshape.168
  1941.4 1.9 collective-permute-start.20
  1943.4 13.5 collective-permute-start.21
  1958.0 3.2 maximum_multiply_fusion
  1967.4 2.0 fusion.25
  1970.1 1.9 collective-permute-start.22
  1972.0 3.6 collective-permute-done.22
  1975.5 1.9 collective-permute-start.23
  1977.5 4.4 collective-permute-done.23
  1981.9 1.9 collective-permute-start.24
  1983.8 7.5 collective-permute-done.24
  1993.2 3.6 collective-permute-done.25
  1996.8 45.7 %collective-permute-start.26 = (f32[4,128]{1,0:T(4,128)S(1)}, f32[4,128]{1,0:T(4,128)S(1)}, u32[]{:S(2)}, u32[]{:S(2)}) collective-permute-start(f32[4,128]{1,0:T(4,128)S(1)} %collective-permute-done.25), channel_id=1, source_target_pairs={{0,64},{4,68},{8,72},{12,76},{16,80},{20,84},{24,88},{28,92},{32,9... | collective-permute-start | bytes 6152 | tf_op jit(solution)/shard_map/ppermute | solution.py:30
  2045.9 3.6 collective-permute-done.27
  2049.5 9.9 collective-permute-start.28
  2062.0 422.9 %all-reduce.3.cloned.1.call-done = f32[589824]{0:T(1024)} async-done(((f32[589824]{0:T(1024)}), f32[589824]{0:T(1024)}) %all-reduce.3.cloned.1.call-update) | async-done | bytes 2359312
  (236 shorter events, 68.6 us)
Async XLA Ops:
  7.2 509.8 %copy-start.37 = (bf16[3,768]{1,0:T(4,128)(2,1)S(1)}, bf16[3,768]{1,0:T(4,128)(2,1)}, u32[]{:S(2)}) copy-start(bf16[3,768]{1,0:T(4,128)(2,1)} %param.14) | copy-start | bytes 13828
  7.2 1150.1 %all-gather.5.cloned.1.call-start = ((), (), s32[]{:S(2)}) async-start(), calls=%async_computation | async-start | bytes 2377728 | tf_op jit(solution)/shard_map/all_gather | solution.py:50
  8.6 1866.7 %all-gather.7.cloned.1.call-start = ((), (), s32[]{:S(2)}) async-start(), calls=%async_computation.1 | async-start | bytes 2377728 | tf_op jit(solution)/shard_map/all_gather | solution.py:50
  10.1 9.9 collective-permute-start.7
  14.0 983.7 %copy-start.22 = (f32[4,768]{1,0:T(4,128)S(1)}, f32[4,768]{1,0:T(4,128)}, u32[]{:S(2)}) copy-start(f32[4,768]{1,0:T(4,128)} %param.15) | copy-start | bytes 36868
  16.6 1081.5 %collective-permute-start = (bf16[128,768]{1,0:T(8,128)(2,1)S(1)}, bf16[128,768]{1,0:T(8,128)(2,1)S(1)}, u32[]{:S(2)}, u32[]{:S(2)}) collective-permute-start(bf16[128,768]{1,0:T(8,128)(2,1)S(1)} %fusion.38), channel_id=1, source_target_pairs={{0,4},{4,0},{8,12},{12,8},{16,20},{20,16},{24,28},{28,24},{32,36},... | collective-permute-start | bytes 589832 | tf_op jit(solution)/shard_map/ppermute | solution.py:30
  20.0 2464.9 %all-reduce.3.cloned.1.call-start = ((), (), s32[]{:S(2)}) async-start(), calls=%async_computation.2 | async-start | bytes 4718592
  20.0 495.0 %collective-permute-start.8 = (bf16[2,128]{1,0:T(2,128)(2,1)S(1)}, bf16[2,128]{1,0:T(2,128)(2,1)S(1)}, u32[]{:S(2)}, u32[]{:S(2)}) collective-permute-start(bf16[2,128]{1,0:T(2,128)(2,1)S(1)} %collective-permute-done.7), channel_id=1, source_target_pairs={{0,8},{4,12},{8,0},{12,4},{16,24},{20,28},{24,16},{28,20},{32,40},... | collective-permute-start | bytes 1544 | tf_op jit(solution)/shard_map/ppermute | solution.py:30
  515.0 480.8 %collective-permute-start.9 = (bf16[2,128]{1,0:T(2,128)(2,1)S(1)}, bf16[2,128]{1,0:T(2,128)(2,1)S(1)}, u32[]{:S(2)}, u32[]{:S(2)}) collective-permute-start(bf16[2,128]{1,0:T(2,128)(2,1)S(1)} %collective-permute-done.8), channel_id=1, source_target_pairs={{0,16},{4,20},{8,24},{12,28},{16,0},{20,4},{24,8},{28,12},{32,48},... | collective-permute-start | bytes 1544 | tf_op jit(solution)/shard_map/ppermute | solution.py:30
  995.8 5.5 collective-permute-start.10
  997.8 168.0 %copy-start.24 = (f32[768]{0:T(1024)}, f32[768]{0:T(1024)S(1)}, u32[]{:S(2)}) copy-start(f32[768]{0:T(1024)S(1)} %get-tuple-element.3) | copy-start | bytes 9220
  997.8 168.0 %copy-start.26 = (f32[768]{0:T(1024)}, f32[768]{0:T(1024)S(1)}, u32[]{:S(2)}) copy-start(f32[768]{0:T(1024)S(1)} %get-tuple-element.4) | copy-start | bytes 9220
  997.8 168.0 %copy-start.28 = (f32[768]{0:T(1024)}, f32[768]{0:T(1024)S(1)}, u32[]{:S(2)}) copy-start(f32[768]{0:T(1024)S(1)} %get-tuple-element.5) | copy-start | bytes 9220
  999.7 97.8 %copy-start.50 = (s32[1,128]{1,0:T(1,128)S(1)}, s32[1,128]{1,0:T(1,128)}, u32[]{:S(2)}) copy-start(s32[1,128]{1,0:T(1,128)} %param.8) | copy-start | bytes 1540
  1000.2 165.6 %copy-start.19 = (bf16[384,768,1]{1,0,2:T(8,128)(2,1)}, bf16[384,768,1]{1,0,2:T(8,128)(2,1)S(1)}, u32[]{:S(2)}) copy-start(bf16[384,768,1]{1,0,2:T(8,128)(2,1)S(1)} %reshape.174) | copy-start | bytes 1769476
  1001.3 45.8 %collective-permute-start.11 = (bf16[2,128]{1,0:T(2,128)(2,1)S(1)}, bf16[2,128]{1,0:T(2,128)(2,1)S(1)}, u32[]{:S(2)}, u32[]{:S(2)}) collective-permute-start(bf16[2,128]{1,0:T(2,128)(2,1)S(1)} %collective-permute-done.10), channel_id=1, source_target_pairs={{0,64},{4,68},{8,72},{12,76},{16,80},{20,84},{24,88},{28,92},{32,9... | collective-permute-start | bytes 1544 | tf_op jit(solution)/shard_map/ppermute | solution.py:30
  1047.1 5.5 collective-permute-start.12
  1049.1 81.2 %copy-start.47 = (bf16[160]{0:T(256)(128)(2,1)}, bf16[160]{0:T(256)(128)(2,1)S(1)}, u32[]{:S(2)}) copy-start(bf16[160]{0:T(256)(128)(2,1)S(1)} %pad.29.clone) | copy-start | bytes 964
  1052.5 43.5 %collective-permute-start.13 = (bf16[2,128]{1,0:T(2,128)(2,1)S(1)}, bf16[2,128]{1,0:T(2,128)(2,1)S(1)}, u32[]{:S(2)}, u32[]{:S(2)}) collective-permute-start(bf16[2,128]{1,0:T(2,128)(2,1)S(1)} %collective-permute-done.12), channel_id=1, source_target_pairs={{0,256},{4,260},{8,264},{12,268},{16,272},{20,276},{24,280},{28,28... | collective-permute-start | bytes 1544 | tf_op jit(solution)/shard_map/ppermute | solution.py:30
  1097.5 68.3 %copy-start.30 = (f32[2,128]{1,0:T(2,128)}, f32[2,128]{1,0:T(2,128)S(1)}, u32[]{:S(2)}) copy-start(f32[2,128]{1,0:T(2,128)S(1)} %fusion.53) | copy-start | bytes 3076
  1097.5 68.3 %copy-start.38 = (pred[2,128]{1,0:T(4,128)(4,1)}, pred[2,128]{1,0:T(4,128)(4,1)S(1)}, u32[]{:S(2)}) copy-start(pred[2,128]{1,0:T(4,128)(4,1)S(1)} %get-tuple-element.36) | copy-start | bytes 772
  1097.5 68.3 %copy-start.40 = (pred[2,128]{1,0:T(4,128)(4,1)}, pred[2,128]{1,0:T(4,128)(4,1)S(1)}, u32[]{:S(2)}) copy-start(pred[2,128]{1,0:T(4,128)(4,1)S(1)} %get-tuple-element.37) | copy-start | bytes 772
  1097.5 68.3 %copy-start.42 = (pred[2,128]{1,0:T(4,128)(4,1)}, pred[2,128]{1,0:T(4,128)(4,1)S(1)}, u32[]{:S(2)}) copy-start(pred[2,128]{1,0:T(4,128)(4,1)S(1)} %get-tuple-element.38) | copy-start | bytes 772
  1097.5 68.3 %copy-start.44 = (pred[2,128]{1,0:T(4,128)(4,1)}, pred[2,128]{1,0:T(4,128)(4,1)S(1)}, u32[]{:S(2)}) copy-start(pred[2,128]{1,0:T(4,128)(4,1)S(1)} %get-tuple-element.39) | copy-start | bytes 772
  1098.1 11.3 collective-permute-start.1
  1109.4 17.9 collective-permute-start.2
  1111.3 18.9 collective-permute-start.14
  1113.7 33.7 %collective-permute-start.15 = (bf16[2,16,768]{2,1,0:T(8,128)(2,1)S(1)}, bf16[2,16,768]{2,1,0:T(8,128)(2,1)S(1)}, u32[]{:S(2)}, u32[]{:S(2)}) collective-permute-start(bf16[2,16,768]{2,1,0:T(8,128)(2,1)S(1)} %slice.285), channel_id=1, source_target_pairs={{4,0},{8,4},{12,8},{16,12},{20,16},{24,20},{28,24},{32,28},{36,32}... | collective-permute-start | bytes 147464 | tf_op jit(solution)/shard_map/ppermute | solution.py:24
  1127.3 7.6 collective-permute-start.3
  1134.8 9.3 collective-permute-start.4
  1144.1 7.7 collective-permute-start.5
  1151.8 748.5 %collective-permute-start.6 = (bf16[128,768]{1,0:T(8,128)(2,1)}, bf16[128,768]{1,0:T(8,128)(2,1)}, u32[]{:S(2)}, u32[]{:S(2)}) collective-permute-start(bf16[128,768]{1,0:T(8,128)(2,1)} %collective-permute-done.5), channel_id=1, source_target_pairs={{0,256},{4,260},{8,264},{12,268},{16,272},{20,276},{24,280},{28,28... | collective-permute-start | bytes 589832 | tf_op jit(solution)/shard_map/ppermute | solution.py:30
  1167.4 714.5 %copy-start.7 = (bf16[2,128,768]{2,1,0:T(8,128)(2,1)}, bf16[2,128,768]{2,1,0:T(8,128)(2,1)S(1)}, u32[]{:S(2)}) copy-start(bf16[2,128,768]{2,1,0:T(8,128)(2,1)S(1)} %get-tuple-element.40) | copy-start | bytes 1179652
  1168.3 719.5 %collective-permute-start.16 = (bf16[2,64,768]{2,1,0:T(8,128)(2,1)}, bf16[2,64,768]{2,1,0:T(8,128)(2,1)}, u32[]{:S(2)}, u32[]{:S(2)}) collective-permute-start(bf16[2,64,768]{2,1,0:T(8,128)(2,1)} %pad_maximum_fusion.1), channel_id=1, source_target_pairs={{0,4},{4,8},{8,12},{12,16},{16,20},{20,24},{24,28},{28,32},{32,36}... | collective-permute-start | bytes 589832 | tf_op jit(solution)/shard_map/ppermute | solution.py:21
  1882.0 8.7 collective-permute-start.17
  1896.7 2.6 copy-start.9
  1904.3 20.5 collective-permute-start.18
  1906.2 20.5 collective-permute-start.19
  1934.7 2.7 copy-start.12
  1941.4 19.8 collective-permute-start.20
  1943.4 19.4 collective-permute-start.21
  1970.1 5.5 collective-permute-start.22
  1975.5 6.4 collective-permute-start.23
  1981.9 9.4 collective-permute-start.24
  1991.3 5.5 collective-permute-start.25
  1996.8 47.3 %collective-permute-start.26 = (f32[4,128]{1,0:T(4,128)S(1)}, f32[4,128]{1,0:T(4,128)S(1)}, u32[]{:S(2)}, u32[]{:S(2)}) collective-permute-start(f32[4,128]{1,0:T(4,128)S(1)} %collective-permute-done.25), channel_id=1, source_target_pairs={{0,64},{4,68},{8,72},{12,76},{16,80},{20,84},{24,88},{28,92},{32,9... | collective-permute-start | bytes 6152 | tf_op jit(solution)/shard_map/ppermute | solution.py:30
  2044.0 5.5 collective-permute-start.27
  2049.5 11.5 collective-permute-start.28
  (35 other events, 49.0 us)
Sparse Core Ops, SparseCore 0:
  10.1 904.1 all-gather.4
  916.3 958.9 all-gather.6
  1961.3 523.5 all-reduce.2
where the time goes:
time: 2490 us
  waiting for transfers between devices  1180 us (47%)
  blocking collectives  969 us (39%)
  starting transfers between devices  240 us (10%)
  local copies, waits for them, and re-layouts  46 us (2%)
    all_gather x2, blocking collectives, fetch(): lax.all_gather(proj_shard, 'seq', axis=0, tiled=True)  969 us
    all_gather x2, waiting for transfers between devices, fetch(): lax.all_gather(conv_shard, 'seq', axis=1, tiled=True)  705 us
    unnamed x4, waiting for transfers between devices  423 us
    ppermute x21, starting transfers between devices, from_partner(): lax.ppermute(array, axis, [(i, i ^ 1 << bit) for i in range(lax.axis_size...  186 us
    ppermute x21, waiting for transfers between devices, from_partner(): lax.ppermute(array, axis, [(i, i ^ 1 << bit) for i in range(lax.axis_size...  55.6 us
  transfers between devices with their start and end apart: 32, of which 17 were waited for; matrix products, arithmetic and copies ran while one was open for 2% of the time, Pallas kernels for 0%

commit v1 on v0

v1 whole, which is shorter than its diff:
```python
import math

import jax
import jax.numpy as jnp
import numpy as np
from jax import lax
from jax.experimental import pallas as pl
from jax.experimental.pallas import tpu as pltpu
from jax.sharding import PartitionSpec as P

MESH = pl.DeviceIdType.MESH
F32 = jnp.float32
BF16 = jnp.bfloat16
C = 768
B = 384
CAP = 128
SQRT_HALF = 0.7071067811865476
INV_SQRT_TWO_PI = 0.3989422804014327
CORE_SUM = BF16
FIRST_SUM = BF16
FAR = 1.0e6


def shard_order():
    table = np.zeros((192, 256), np.float32)
    for row in range(192):
        piece, within = divmod(row, 48)
        if piece < 3:
            source = within // 6 * 32 + piece * 6 + within % 6
        else:
            half, rest = divmod(within, 24)
            source = rest // 3 * 32 + 18 + half * 3 + rest % 3
        table[row, source] = 1.0
    return table


def class_order():
    table = np.zeros((B, B), np.float32)
    for row in range(B):
        table[row, row % 3 * 128 + row // 3] = 1.0
    return table


def triple_codes():
    table = np.zeros((128, 128), np.float32)
    for row in range(125):
        table[row, :3] = row // 25, row // 5 % 5, row % 5
    return table


def gelu_pair(values):
    bell = 1.0 + lax.erf(values * SQRT_HALF)
    slope = 0.5 * bell + values * jnp.exp(-0.5 * values * values) * INV_SQRT_TWO_PI
    return 0.5 * values * bell, slope


def dot(left, right):
    return jnp.dot(left, right, preferred_element_type=F32)


def dot_nt(left, right):
    return lax.dot_general(left, right, (((1,), (1,)), ((), ())), preferred_element_type=F32)


def dot_tn(left, right):
    return lax.dot_general(left, right, (((0,), (0,)), ((), ())), preferred_element_type=F32)


def halves(values):
    high = values.astype(BF16)
    return high, (values - high.astype(F32)).astype(BF16)


def pick(onehot, pair):
    return dot(onehot, pair[0]) + dot(onehot, pair[1])


def ones_where(mask):
    return jnp.where(mask, 1.0, 0.0)


def iota(shape, dim):
    return lax.broadcasted_iota(jnp.int32, shape, dim)


def kernel(
    bases_ref,
    len_ref,
    cot_ref,
    conv1_ref,
    proj1_ref,
    conv2_ref,
    proj2_ref,
    embed_ref,
    order_ref,
    class_ref,
    codes_ref,
    sal_ref,
    grad_ref,
    pack32,
    shard,
    zbuf,
    weights,
    tail,
    left_rows,
    right_rows,
    enc_own,
    enc_all,
    emb_fwd,
    emb_rev,
    send0,
    recv0,
    acc0,
    part_f32,
    part_low,
    recv1,
    part2,
    recv2,
    part3,
    recv3,
    send_sem,
    recv_sem,
):
    seq = lax.axis_index("seq")
    dpi = lax.axis_index("dp")
    x, y, zl = seq // 32, seq // 8 % 4, seq % 8
    zh, core = dpi // 2, dpi % 2
    z = zh * 8 + zl
    other = 1 - core
    one = y + core * (x - y)
    two = x + core * (y - x)

    def chip(first, second):
        cx = second + core * (first - second)
        cy = first + core * (second - first)
        return ((cx * 4 + cy) * 8 + zl, dpi)

    def along_z(target):
        return ((x * 4 + y) * 8 + target % 8, target // 8 * 2 + core)

    def along_seq(offset):
        return ((seq + offset + 128) % 128, dpi)

    sibling = (seq, zh * 2 + other)

    barrier = pltpu.get_barrier_semaphore()
    partners = [sibling]
    partners += [chip((one + k) % 4, two) for k in (1, 2, 3)]
    partners += [chip(one, (two + k) % 4) for k in (1, 2, 3)]
    partners += [along_z((z + k) % 16) for k in range(1, 16)]
    partners += [along_seq(k) for k in (-3, -2, -1, 1, 2, 3)]
    for device in partners:
        pl.semaphore_signal(barrier, inc=1, device_id=device, device_id_type=MESH)

    used = {"send": 0}
    started = []

    def push(source, target, slot, device):
        copy = pltpu.make_async_remote_copy(
            src_ref=source,
            dst_ref=target,
            send_sem=send_sem.at[used["send"]],
            recv_sem=recv_sem.at[slot],
            device_id=device,
            device_id_type=MESH,
        )
        used["send"] += 1
        copy.start()
        started.append(copy)

    def arrive(target, slot):
        pltpu.make_async_remote_copy(
            src_ref=target,
            dst_ref=target,
            send_sem=send_sem.at[0],
            recv_sem=recv_sem.at[slot],
            device_id=sibling,
            device_id_type=MESH,
        ).wait_recv()

    lane = iota((1, CAP), 1)
    live_count = len_ref[...]
    code_row = jnp.where(lane < live_count, bases_ref[...] + 1, 0).astype(F32)
    enc_own[...] = jnp.broadcast_to(code_row, (8, CAP))
    own_cot = cot_ref[0]
    choose = iota((80, CAP), 1) - iota((80, CAP), 0) == live_count - 80
    tail[...] = dot(ones_where(choose).astype(BF16), own_cot).astype(BF16)
    left_rows[96:128] = jnp.zeros((32, C), BF16)
    right_rows[96:128] = jnp.zeros((32, C), BF16)
    first_core = core == 0
    for k in range(3):
        pack32[6 * k : 6 * k + 6] = jnp.where(
            first_core, conv1_ref[k].astype(F32), conv2_ref[k].astype(F32)
        )
    proj_rows = jnp.where(first_core, proj1_ref[...].astype(F32), proj2_ref[...].astype(F32))
    pack32[18:21] = proj_rows[:, :B]
    pack32[21:24] = proj_rows[:, B:]
    pack32[24:32] = jnp.zeros((8, B), F32)
    shard[...] = pack32[...].astype(BF16)
    zbuf[zl] = pack32[...].astype(BF16)
    emb_fwd[0:4] = embed_ref[...]
    emb_fwd[4:8] = jnp.zeros((4, C), F32)
    emb_rev[4:8] = jnp.zeros((4, C), F32)
    for k in range(4):
        emb_rev[k : k + 1] = embed_ref[3 - k : 4 - k]

    pl.semaphore_wait(barrier, len(partners))

    Z, D1F, D1H, D2F, D2H, SIB, HALO, ENC, R0, R1, R2, R3 = (
        0, 8, 10, 12, 20, 28, 44, 48, 54, 56, 60, 64,
    )
    z_offsets = [1, 15, 2, 14, 3, 13, 4 + 8 * core]
    for offset in z_offsets:
        push(shard, zbuf.at[zl], Z + zl, along_z((z + offset) % 16))
    for k in (1, 2, 3):
        push(enc_own, enc_all.at[k - 1], ENC + k - 1, along_seq(k))
        push(enc_own, enc_all.at[2 + k], ENC + 2 + k, along_seq(-k))
    for k in range(1, 8):
        arrive(zbuf.at[(zl + k) % 8], Z + (zl + k) % 8)
    push(tail, left_rows.at[0:80], HALO, along_seq(1))
    push(cot_ref.at[0, 0:80], right_rows.at[0:80], HALO + 1, along_seq(-1))
    push(tail.at[64:80], left_rows.at[80:96], HALO + 2, along_seq(2))
    push(cot_ref.at[0, 0:16], right_rows.at[80:96], HALO + 3, along_seq(-2))

    def block_of(owner, first, second, piece, count):
        group = first * (1 + 3 * owner) + second * (4 - 3 * owner)
        rows = pl.ds(pl.multiple_of(group * 48, 16), 48)
        return weights.at[pl.ds(4 * owner + piece, count), rows, :]

    moved = dot(order_ref[...], zbuf[...].reshape(256, B)).astype(BF16)
    own_rows = pl.ds(pl.multiple_of((x * 4 + y) * 48, 16), 48)
    for k in range(4):
        weights[4 * core + k, own_rows, :] = moved[48 * k : 48 * k + 48]

    steps = (0, 3, 1, 2)

    def line(step, turn, piece=0, count=4):
        return block_of(core, (one + steps[step]) % 4, (two + steps[turn]) % 4, piece, count)

    one_up, one_down = chip((one + 1) % 4, two), chip((one + 3) % 4, two)
    two_up, two_down = chip(one, (two + 1) % 4), chip(one, (two + 3) % 4)

    def to_sibling(step, turn):
        push(line(step, turn), line(step, turn), SIB + step * 4 + turn, sibling)

    def to_second(step):
        push(line(step, 0), line(step, 0), D2F + step * 2, two_up)
        push(line(step, 0), line(step, 0), D2F + step * 2 + 1, two_down)

    def relay_second(step):
        arrive(line(step, 1), D2F + step * 2)
        push(line(step, 1, 0, 2), line(step, 1, 0, 2), D2H + step * 2, two_up)
        to_sibling(step, 1)
        arrive(line(step, 2), D2F + step * 2 + 1)
        push(line(step, 2, 2, 2), line(step, 2, 2, 2), D2H + step * 2 + 1, two_down)
        to_sibling(step, 2)

    push(line(0, 0), line(0, 0), D1F, one_up)
    push(line(0, 0), line(0, 0), D1F + 1, one_down)
    to_second(0)
    to_sibling(0, 0)
    arrive(line(1, 0), D1F)
    push(line(1, 0, 0, 2), line(1, 0, 0, 2), D1H, one_up)
    to_second(1)
    to_sibling(1, 0)
    arrive(line(2, 0), D1F + 1)
    push(line(2, 0, 2, 2), line(2, 0, 2, 2), D1H + 1, one_down)
    to_second(2)
    to_sibling(2, 0)
    relay_second(0)
    arrive(line(3, 0, 0, 2), D1H)
    arrive(line(3, 0, 2, 2), D1H + 1)
    to_second(3)
    to_sibling(3, 0)
    for step in (1, 2, 3):
        relay_second(step)
    for step in range(4):
        arrive(line(step, 3, 0, 2), D2H + step * 2)
        arrive(line(step, 3, 2, 2), D2H + step * 2 + 1)
        to_sibling(step, 3)

    for k in range(6):
        arrive(enc_all.at[k], ENC + k)
    own_n = jnp.sum(ones_where(code_row > 0.0), axis=1, keepdims=True)
    lane_f = lane.astype(F32)
    rows_t = (iota((448, 1), 0) - 160).astype(F32)
    pieces = [(code_row, jnp.zeros((1, 1), F32))]
    left_n, right_n = [], []
    left_at, right_at = jnp.zeros((1, 1), F32), own_n
    for k in (1, 2, 3):
        there = jnp.where(seq >= k, 1.0, 0.0)
        row = enc_all[k - 1, 0:1] * there
        count = jnp.sum(ones_where(row > 0.0), axis=1, keepdims=True)
        left_at = left_at - count
        left_n.append(count)
        pieces.append((row, left_at))
        there = jnp.where(seq + k <= 127, 1.0, 0.0)
        row = enc_all[2 + k, 0:1] * there
        count = jnp.sum(ones_where(row > 0.0), axis=1, keepdims=True)
        pieces.append((row, right_at))
        right_at = right_at + count
        right_n.append(count)
    found = jnp.zeros((448, CAP), F32)
    for row, start in pieces:
        found = found + jnp.where(rows_t == lane_f + start, row, 0.0)
    code = jnp.sum(found, axis=1, keepdims=True)
    flip = jnp.where(code > 0.0, 5.0 - code, 0.0)
    triple_f = 25.0 * code[0:416] + 5.0 * code[16:432] + code[32:448]
    triple_r = 25.0 * flip[32:448] + 5.0 * flip[16:432] + flip[0:416]
    hot_f = ones_where(triple_f == lane_f).astype(BF16)
    hot_r = ones_where(triple_r == lane_f).astype(BF16)

    arrive(left_rows.at[0:80], HALO)
    arrive(right_rows.at[0:80], HALO + 1)
    arrive(left_rows.at[80:96], HALO + 2)
    arrive(right_rows.at[80:96], HALO + 3)
    t288 = (iota((288, 1), 0) - 80).astype(F32)
    own_pos = jnp.where(lane_f < own_n, lane_f, FAR)
    left_pos = jnp.where(lane_f >= 80.0 - left_n[0], lane_f - 80.0, FAR)
    left_far = jnp.where(left_n[1] > 0.0, lane_f - 96.0 - left_n[0], FAR)
    left_pos = jnp.where(lane_f < 80.0, left_pos, jnp.where(lane_f < 96.0, left_far, FAR))
    right_pos = jnp.where(lane_f < right_n[0], lane_f + own_n, FAR)
    right_far = jnp.where(right_n[1] > 0.0, lane_f - 80.0 + own_n + right_n[0], FAR)
    right_pos = jnp.where(lane_f < 80.0, right_pos, jnp.where(lane_f < 96.0, right_far, FAR))
    cot = (
        dot(ones_where(t288 == own_pos).astype(BF16), own_cot)
        + dot(ones_where(t288 == left_pos).astype(BF16), left_rows[...])
        + dot(ones_where(t288 == right_pos).astype(BF16), right_rows[...])
    )
    grad2 = 0.5 * cot
    grad2_low = grad2.astype(BF16)

    for step in range(4):
        for turn in range(4):
            theirs = block_of(
                other,
                (x + core * (y - x) + steps[step]) % 4,
                (y + core * (x - y) + steps[turn]) % 4,
                0,
                4,
            )
            arrive(theirs, SIB + step * 4 + turn)

    def projection(block):
        rows = weights[4 * block + 3].astype(F32).reshape(16, 2, 24, B)
        return [rows[:, half].reshape(B, B).astype(BF16) for half in range(2)]

    proj1 = jnp.concatenate(projection(0), axis=1)
    proj2 = jnp.concatenate(projection(1), axis=1)

    before_code, mid_code, after_code = codes_ref[:, 0:1], codes_ref[:, 1:2], codes_ref[:, 2:3]
    value0, slope0 = gelu_pair(emb_fwd[...])
    low0 = value0.astype(BF16)
    hidden1 = jnp.zeros((128, B), F32)
    for k, column in enumerate((before_code, mid_code, after_code)):
        rows = dot(low0, weights[k])
        for base in range(4):
            hidden1 = hidden1 + jnp.where(column == base + 1.0, rows[base : base + 1], 0.0)
    table_live = ones_where(mid_code > 0.0)
    hidden1 = hidden1 * table_live
    value1, slope1 = gelu_pair(hidden1)
    mid1 = value1.astype(BF16)
    slope1 = halves(slope1 * table_live)
    stream1 = jnp.zeros((128, C), F32)
    for base in range(4):
        stream1 = stream1 + jnp.where(mid_code == base + 1.0, emb_fwd[base : base + 1], 0.0)
    stream1 = stream1 + dot(mid1, proj1)
    value_x, slope_x = gelu_pair(stream1)
    low_x = (value_x * table_live).astype(BF16)
    slope_x = halves(slope_x * table_live)
    taps2 = halves(jnp.concatenate([dot(low_x, weights[4 + k]) for k in range(3)], axis=0))

    hot2 = jnp.concatenate(
        [
            jnp.concatenate([hot_f[0:288], hot_f[64:352], hot_f[128:416]], axis=1),
            jnp.concatenate([hot_r[128:416], hot_r[64:352], hot_r[0:288]], axis=1),
        ],
        axis=0,
    )
    hidden2 = pick(hot2, taps2)
    value2, slope2 = gelu_pair(hidden2)
    live288 = ones_where(code[80:368] > 0.0)
    back2 = dot_nt(grad2_low, proj2) * live288
    own_mask = ones_where(iota((CAP, 1), 0).astype(F32) < own_n)
    mid2 = jnp.concatenate([value2[80:208] * own_mask, value2[368:496] * own_mask], axis=0)
    classes = class_ref[...]
    mid2 = dot(mid2.astype(BF16), classes).astype(BF16)
    own_grad2 = grad2_low[80:208]
    sum2 = dot_tn(mid2, jnp.concatenate([own_grad2, own_grad2], axis=0))

    def to_core(block, total):
        first = jnp.concatenate([total[0:128], total[128:256, 0:B]], axis=1)
        second = jnp.concatenate([total[128:256, B:], total[256:384]], axis=1)
        send0[block] = jnp.where(first_core, second, first).astype(CORE_SUM).reshape(8, 16, 1152)
        acc0[block] = jnp.where(first_core, first, second).reshape(8, 16, 1152)
        push(send0.at[block], recv0.at[block], R0 + block, sibling)

    to_core(1, sum2)
    gh_f = (back2 * slope2[0:288]).astype(BF16)
    gh_r = (back2 * slope2[288:576]).astype(BF16)
    near2 = [
        jnp.concatenate([gh_f[128:288], gh_r[0:160]], axis=0),
        jnp.concatenate([gh_f[64:224], gh_r[64:224]], axis=0),
        jnp.concatenate([gh_f[0:160], gh_r[128:288]], axis=0),
    ]
    active2 = dot_nt(near2[0], weights[4])
    active2 = active2 + dot_nt(near2[1], weights[5])
    active2 = active2 + dot_nt(near2[2], weights[6])
    hot1 = jnp.concatenate([hot_f[128:288], hot_r[128:288]], axis=0)
    around = grad2[64:224]
    grad1 = jnp.concatenate([around, around], axis=0) + active2 * pick(hot1, slope_x)
    grad1_low = grad1.astype(BF16)

    own_low = own_mask.astype(BF16)
    own_hot = jnp.concatenate([hot_f[144:272] * own_low, hot_r[144:272] * own_low], axis=0)
    mid1 = dot(own_hot, dot(mid1, classes).astype(BF16)).astype(BF16)
    sum1 = dot_tn(mid1, jnp.concatenate([grad1_low[16:144], grad1_low[176:304]], axis=0))
    to_core(0, sum1)
    back1 = dot_nt(grad1_low, proj1)
    gh1 = (back1 * pick(hot1, slope1)).astype(BF16)
    near1 = [
        jnp.concatenate([gh1[32:160], gh1[160:288]], axis=0),
        jnp.concatenate([gh1[16:144], gh1[176:304]], axis=0),
        jnp.concatenate([gh1[0:128], gh1[192:320]], axis=0),
    ]

    for block in (1, 0):
        arrive(recv0.at[block], R0 + block)
        for piece in range(8):
            both = acc0[block, piece] + recv0[block, piece].astype(F32)
            px, py = 2 * block + piece // 4, piece % 4
            first = py + other * (px - py)
            second = px + other * (py - px)
            part_f32[first, second] = both
            part_low[first, second] = both.astype(FIRST_SUM)
    for k in (2, 1, 3):
        goal = (two + k) % 4
        push(part_low.at[goal], recv1.at[two], R1 + two, chip(one, goal))

    active1 = dot_nt(near1[0], weights[0])
    active1 = active1 + dot_nt(near1[1], weights[1])
    active1 = active1 + dot_nt(near1[2], weights[2])
    own_code, own_flip = code[160:288], flip[160:288]
    slope_f = jnp.zeros((CAP, C), F32)
    slope_r = jnp.zeros((CAP, C), F32)
    for base in range(4):
        slope_f = jnp.where(own_code == base + 1.0, slope0[base : base + 1], slope_f)
        slope_r = jnp.where(own_flip == base + 1.0, slope0[base : base + 1], slope_r)
    start_f = grad1[16:144] + active1[0:128] * slope_f
    start_r = grad1[176:304] + active1[128:256] * slope_r
    exact = lax.Precision.HIGHEST
    contract = (((1,), (1,)), ((), ()))
    score = lax.dot_general(
        emb_fwd[...], start_f, contract, precision=exact, preferred_element_type=F32
    ) + lax.dot_general(
        emb_rev[...], start_r, contract, precision=exact, preferred_element_type=F32
    )
    score = jnp.where(lane < live_count, score, 0.0) * (1.0 / math.sqrt(C))
    sal_ref[0] = score[0:4]

    for k in (1, 2, 3):
        source = (two + k) % 4
        arrive(recv1.at[source], R1 + source)
    total = part_f32[two]
    for k in (1, 2, 3):
        total = total + recv1[(two + k) % 4].astype(F32)
    part2[...] = total
    for k in (2, 1, 3):
        goal = (one + k) % 4
        push(part2.at[goal], recv2.at[one], R2 + one, chip(goal, two))
    for k in (1, 2, 3):
        source = (one + k) % 4
        arrive(recv2.at[source], R2 + source)
    total = part2[one]
    for k in (1, 2, 3):
        total = total + recv2[(one + k) % 4]
    for k in range(16):
        part3[k] = total[k : k + 1]
    place = zl * 2 + zh
    for k in (8, 7, 9, 6, 10, 5, 11, 4, 12, 3, 13, 2, 14, 1, 15):
        goal = (z + k) % 16
        push(part3.at[goal % 8 * 2 + goal // 8], recv3.at[place], R3 + place, along_z(goal))
    for k in range(1, 16):
        source = (place + k) % 16
        arrive(recv3.at[source], R3 + source)
    total = part3[place]
    for k in range(1, 16):
        total = total + recv3[(place + k) % 16]
    grad_ref[...] = total * (1.0 / 256.0)

    for copy in started:
        copy.wait_send()


def shards(bases, lengths, cotangent, conv1, proj1, conv2, proj2, embed):
    vmem = pl.BlockSpec(memory_space=pltpu.VMEM)
    saliency, grad = pl.pallas_call(
        kernel,
        out_shape=(
            jax.ShapeDtypeStruct((1, 4, CAP), F32),
            jax.ShapeDtypeStruct((1, 1152), F32),
        ),
        in_specs=[vmem] * 11,
        out_specs=(vmem, vmem),
        scratch_shapes=[
            pltpu.VMEM((32, B), F32),
            pltpu.VMEM((32, B), BF16),
            pltpu.VMEM((8, 32, B), BF16),
            pltpu.VMEM((8, C, B), BF16),
            pltpu.VMEM((80, C), BF16),
            pltpu.VMEM((128, C), BF16),
            pltpu.VMEM((128, C), BF16),
            pltpu.VMEM((8, CAP), F32),
            pltpu.VMEM((6, 8, CAP), F32),
            pltpu.VMEM((8, C), F32),
            pltpu.VMEM((8, C), F32),
            pltpu.VMEM((2, 8, 16, 1152), CORE_SUM),
            pltpu.VMEM((2, 8, 16, 1152), CORE_SUM),
            pltpu.VMEM((2, 8, 16, 1152), F32),
            pltpu.VMEM((4, 4, 16, 1152), F32),
            pltpu.VMEM((4, 4, 16, 1152), FIRST_SUM),
            pltpu.VMEM((4, 4, 16, 1152), FIRST_SUM),
            pltpu.VMEM((4, 16, 1152), F32),
            pltpu.VMEM((4, 16, 1152), F32),
            pltpu.VMEM((16, 1, 1152), F32),
            pltpu.VMEM((16, 1, 1152), F32),
            pltpu.SemaphoreType.DMA((80,)),
            pltpu.SemaphoreType.DMA((80,)),
        ],
        compiler_params=pltpu.CompilerParams(
            collective_id=0, has_side_effects=True, vmem_limit_bytes=60 * 1024 * 1024
        ),
    )(
        bases,
        lengths,
        cotangent,
        conv1,
        proj1,
        conv2,
        proj2,
        embed,
        jnp.asarray(shard_order(), BF16),
        jnp.asarray(class_order(), BF16),
        jnp.asarray(triple_codes(), F32),
    )
    return saliency, grad.reshape(1152)


def solution(mesh):
    in_specs = (
        P("dp", "seq"),
        P("dp", "seq"),
        P("dp", "seq", None),
        P(None, "seq", None),
        P("seq", None),
        P(None, "seq", None),
        P("seq", None),
        P(),
    )
    out_specs = (P("dp", None, "seq"), P(("seq", "dp")))
    return jax.shard_map(shards, mesh=mesh, in_specs=in_specs, out_specs=out_specs, check_vma=False)
```

time: 2490 us -> 76.5 us (0.03)
  waiting for transfers between devices: 1180 us -> 0 us
  blocking collectives: 969 us -> 0 us
  starting transfers between devices: 240 us -> 0 us
  Pallas kernels: 0 us -> 72.3 us
  local copies, waits for them, and re-layouts: 46 us -> 0.58 us
    all_gather x2 -> x0, blocking collectives: 969 us -> none  [fetch(): lax.all_gather(proj_shard, 'seq', axis=0, tiled=True)]
    all_gather x2 -> x0, waiting for transfers between devices: 705 us -> none  [fetch(): lax.all_gather(conv_shard, 'seq', axis=1, tiled=True)]
    unnamed x4 -> x0, waiting for transfers between devices: 423 us -> none
    ppermute x29 -> x0, starting transfers between devices: 240 us -> none  [the longest x21 186 us: from_partner(): lax.ppermute(array, axis, [(i, i ^ 1 << bit) for i in range(lax.axis_size...]
    pallas_call x0 -> x1, Pallas kernels: none -> 72.3 us  [shards(): pl.pallas_call(kernel, out_shape=(jax.ShapeDtypeStruct((1, 4, CAP), F32),...]
    ppermute x29 -> x0, waiting for transfers between devices: 55.6 us -> none  [the longest x21 55.6 us: from_partner(): lax.ppermute(array, axis, [(i, i ^ 1 << bit) for i in range(lax.axis_size...]
  transfers between devices with their start and end apart: 32 -> 0, of which waited for: 17 -> 0; matrix products, arithmetic and copies ran while one was open for 2% -> 0% of each run, Pallas kernels for 0% -> 0%
where the time goes in v1:
time: 76.5 us; the launch traced here: 75.4 us
  Pallas kernels  72.3 us (95%)
  other arithmetic  1.31 us (2%)
  between operations  1.29 us (2%)
    pallas_call x1, Pallas kernels, shards(): pl.pallas_call(kernel, out_shape=(jax.ShapeDtypeStruct((1, 4, CAP), F32),...  72.3 us

profile of v1, /device:TPU:6, one launch (start us, length us, event | category | flops | bytes accessed | tf_op | source)
XLA Modules:
  0.0 75.4 jit_solution(4741584403301210541)
XLA Ops:
  1.3 72.3 %shard_map.122 = (f32[1,4,128]{2,1,0:T(4,128)}, f32[1,1152]{1,0:T(1,128)}) custom-call(s32[1,128]{1,0:T(1,128)} %bases_ref.1, s32[1,1]{1,0:T(1,128)S(6)} %copy.14.len_ref, bf16[1,128,768]{2,1,0:T(8,128)(2,1)} %cot_ref.1, bf16[3,6,384]{2,1,0:T(8,128)(2,1)} %conv1_ref.1, bf16[3,768]{1,0:T(4,128)(2,1)} %proj1_ref.1, bf16[3,6,384]{2,1,0:T(8,128)(2,1)} %conv2_ref.1, ...), custom_call_target="tpu_custom_call" | custom-call | tf_op jit(solution)/shard_map/pallas_call | solution.py:497
  73.5 0.0 copy-start
  73.6 1.3 %reduce = f32[1152]{0:T(1024)} reduce(f32[1,1152]{1,0:T(1,128)} %get-tuple-element.5, f32[]{:T(128)} %constant.16), dimensions={0}, to_apply=%get-tuple-element.5.reduce_sub_computation | reduce | bytes 9220 | tf_op jit(solution)/shard_map/pallas_call | solution.py:497
  74.9 0.0 copy-done
  74.9 0.6 copy.15
Async XLA Ops:
  73.5 1.3 %copy-start = (f32[1,4,128]{2,1,0:T(4,128)S(1)}, f32[1,4,128]{2,1,0:T(4,128)}, u32[]{:S(2)}) copy-start(f32[1,4,128]{2,1,0:T(4,128)} %get-tuple-element.8) | copy-start | bytes 6148

commit v2 on v1

--- a/solution.py
+++ b/solution.py
@@ -18,18 +18,19 @@
 INV_SQRT_TWO_PI = 0.3989422804014327
 CORE_SUM = BF16
 FIRST_SUM = BF16
+SECOND_SUM = BF16
 FAR = 1.0e6
 
 
 def shard_order():
-    table = np.zeros((192, 256), np.float32)
+    table = np.zeros((192, 192), np.float32)
     for row in range(192):
         piece, within = divmod(row, 48)
         if piece < 3:
-            source = within // 6 * 32 + piece * 6 + within % 6
+            source = within // 6 * 24 + piece * 6 + within % 6
         else:
             half, rest = divmod(within, 24)
-            source = rest // 3 * 32 + 18 + half * 3 + rest % 3
+            source = rest // 3 * 24 + 18 + half * 3 + rest % 3
         table[row, source] = 1.0
     return table
 
@@ -84,6 +85,19 @@
 
 
 def kernel(
+    bases_hbm,
+    len_hbm,
+    cot_hbm,
+    conv1_hbm,
+    proj1_hbm,
+    conv2_hbm,
+    proj2_hbm,
+    embed_hbm,
+    order_hbm,
+    class_hbm,
+    codes_hbm,
+    sal_ref,
+    grad_ref,
     bases_ref,
     len_ref,
     cot_ref,
@@ -95,8 +109,6 @@
     order_ref,
     class_ref,
     codes_ref,
-    sal_ref,
-    grad_ref,
     pack32,
     shard,
     zbuf,
@@ -116,10 +128,13 @@
     recv1,
     part2,
     recv2,
+    part2_f32,
     part3,
     recv3,
     send_sem,
     recv_sem,
+    copy_sem,
+    known_sem,
 ):
     seq = lax.axis_index("seq")
     dpi = lax.axis_index("dp")
@@ -144,13 +159,43 @@
     sibling = (seq, zh * 2 + other)
 
     barrier = pltpu.get_barrier_semaphore()
-    partners = [sibling]
-    partners += [chip((one + k) % 4, two) for k in (1, 2, 3)]
-    partners += [chip(one, (two + k) % 4) for k in (1, 2, 3)]
-    partners += [along_z((z + k) % 16) for k in range(1, 16)]
-    partners += [along_seq(k) for k in (-3, -2, -1, 1, 2, 3)]
+    line_x = [(((x + k) % 4 * 4 + y) * 8 + zl, dpi) for k in (1, 3)]
+    line_y = [((x * 4 + (y + k) % 4) * 8 + zl, dpi) for k in (1, 3)]
+    near_z = [along_z((z + k) % 16) for k in (2, 14)]
+    far_z = [along_z((z + k) % 16) for k in (4, 12)]
+    partners = [sibling] + line_x + line_y + near_z
+    partners += [along_z((z + k) % 16) for k in (1, 15)]
     for device in partners:
         pl.semaphore_signal(barrier, inc=1, device_id=device, device_id_type=MESH)
+
+    loads = []
+    for k, (source, target) in enumerate(
+        (
+            (conv1_hbm, conv1_ref),
+            (conv2_hbm, conv2_ref),
+            (proj1_hbm, proj1_ref),
+            (proj2_hbm, proj2_ref),
+            (len_hbm, len_ref),
+            (bases_hbm, bases_ref),
+            (embed_hbm, embed_ref),
+            (cot_hbm, cot_ref),
+            (order_hbm, order_ref),
+            (class_hbm, class_ref),
+            (codes_hbm, codes_ref),
+        )
+    ):
+        copy = pltpu.make_async_copy(source, target, copy_sem.at[k])
+        copy.start()
+        loads.append(copy)
+
+    def announce(devices, slot):
+        for device in devices:
+            pl.semaphore_signal(
+                known_sem.at[slot], inc=1, device_id=device, device_id_type=MESH
+            )
+
+    def heard(slot):
+        pl.semaphore_wait(known_sem.at[slot], 2)
 
     used = {"send": 0}
     started = []
@@ -178,8 +223,10 @@
             device_id_type=MESH,
         ).wait_recv()
 
+    for copy in loads:
+        copy.wait()
     lane = iota((1, CAP), 1)
-    live_count = len_ref[...]
+    live_count = len_ref[0, 0]
     code_row = jnp.where(lane < live_count, bases_ref[...] + 1, 0).astype(F32)
     enc_own[...] = jnp.broadcast_to(code_row, (8, CAP))
     own_cot = cot_ref[0]
@@ -195,7 +242,6 @@
     proj_rows = jnp.where(first_core, proj1_ref[...].astype(F32), proj2_ref[...].astype(F32))
     pack32[18:21] = proj_rows[:, :B]
     pack32[21:24] = proj_rows[:, B:]
-    pack32[24:32] = jnp.zeros((8, B), F32)
     shard[...] = pack32[...].astype(BF16)
     zbuf[zl] = pack32[...].astype(BF16)
     emb_fwd[0:4] = embed_ref[...]
@@ -209,25 +255,40 @@
     Z, D1F, D1H, D2F, D2H, SIB, HALO, ENC, R0, R1, R2, R3 = (
         0, 8, 10, 12, 20, 28, 44, 48, 54, 56, 60, 64,
     )
-    z_offsets = [1, 15, 2, 14, 3, 13, 4 + 8 * core]
-    for offset in z_offsets:
-        push(shard, zbuf.at[zl], Z + zl, along_z((z + offset) % 16))
-    for k in (1, 2, 3):
-        push(enc_own, enc_all.at[k - 1], ENC + k - 1, along_seq(k))
-        push(enc_own, enc_all.at[2 + k], ENC + 2 + k, along_seq(-k))
-    for k in range(1, 8):
-        arrive(zbuf.at[(zl + k) % 8], Z + (zl + k) % 8)
-    push(tail, left_rows.at[0:80], HALO, along_seq(1))
-    push(cot_ref.at[0, 0:80], right_rows.at[0:80], HALO + 1, along_seq(-1))
-    push(tail.at[64:80], left_rows.at[80:96], HALO + 2, along_seq(2))
-    push(cot_ref.at[0, 0:16], right_rows.at[80:96], HALO + 3, along_seq(-2))
+    turn_z = 1 - 2 * core
+
+    def z_at(offset):
+        return along_z((z + offset * turn_z + 16) % 16)
+
+    def z_slot(offset):
+        return (zl + offset * turn_z + 8) % 8
+
+    def z_wait(offset):
+        arrive(zbuf.at[z_slot(offset)], Z + z_slot(offset))
+
+    def z_pass(offset, onward):
+        z_wait(offset)
+        held = zbuf.at[z_slot(offset)]
+        push(held, held, Z + z_slot(offset), z_at(onward))
+
+    for offset in (2, -2, 1, -1):
+        push(shard, zbuf.at[zl], Z + zl, z_at(offset))
+    announce(near_z, 0)
+    z_pass(-1, 2)
+    z_pass(1, -2)
+    z_pass(-2, 2)
+    heard(0)
+    announce(far_z, 1)
+    for offset in (2, 3, -3, -4):
+        z_wait(offset)
 
     def block_of(owner, first, second, piece, count):
         group = first * (1 + 3 * owner) + second * (4 - 3 * owner)
         rows = pl.ds(pl.multiple_of(group * 48, 16), 48)
         return weights.at[pl.ds(4 * owner + piece, count), rows, :]
 
-    moved = dot(order_ref[...], zbuf[...].reshape(256, B)).astype(BF16)
+    gathered = zbuf[...].astype(F32).reshape(192, B).astype(BF16)
+    moved = dot(order_ref[...], gathered).astype(BF16)
     own_rows = pl.ds(pl.multiple_of((x * 4 + y) * 48, 16), 48)
     for k in range(4):
         weights[4 * core + k, own_rows, :] = moved[48 * k : 48 * k + 48]
@@ -259,6 +320,8 @@
     push(line(0, 0), line(0, 0), D1F + 1, one_down)
     to_second(0)
     to_sibling(0, 0)
+    heard(1)
+    announce(line_x, 2)
     arrive(line(1, 0), D1F)
     push(line(1, 0, 0, 2), line(1, 0, 0, 2), D1H, one_up)
     to_second(1)
@@ -267,7 +330,17 @@
     push(line(2, 0, 2, 2), line(2, 0, 2, 2), D1H + 1, one_down)
     to_second(2)
     to_sibling(2, 0)
+    heard(2)
+    announce(line_y, 3)
     relay_second(0)
+    heard(3)
+    for k in (1, 2, 3):
+        push(enc_own, enc_all.at[k - 1], ENC + k - 1, along_seq(k))
+        push(enc_own, enc_all.at[2 + k], ENC + 2 + k, along_seq(-k))
+    push(tail, left_rows.at[0:80], HALO, along_seq(1))
+    push(cot_ref.at[0, 0:80], right_rows.at[0:80], HALO + 1, along_seq(-1))
+    push(tail.at[64:80], left_rows.at[80:96], HALO + 2, along_seq(2))
+    push(cot_ref.at[0, 0:16], right_rows.at[80:96], HALO + 3, along_seq(-2))
     arrive(line(3, 0, 0, 2), D1H)
     arrive(line(3, 0, 2, 2), D1H + 1)
     to_second(3)
@@ -310,26 +383,6 @@
     hot_f = ones_where(triple_f == lane_f).astype(BF16)
     hot_r = ones_where(triple_r == lane_f).astype(BF16)
 
-    arrive(left_rows.at[0:80], HALO)
-    arrive(right_rows.at[0:80], HALO + 1)
-    arrive(left_rows.at[80:96], HALO + 2)
-    arrive(right_rows.at[80:96], HALO + 3)
-    t288 = (iota((288, 1), 0) - 80).astype(F32)
-    own_pos = jnp.where(lane_f < own_n, lane_f, FAR)
-    left_pos = jnp.where(lane_f >= 80.0 - left_n[0], lane_f - 80.0, FAR)
-    left_far = jnp.where(left_n[1] > 0.0, lane_f - 96.0 - left_n[0], FAR)
-    left_pos = jnp.where(lane_f < 80.0, left_pos, jnp.where(lane_f < 96.0, left_far, FAR))
-    right_pos = jnp.where(lane_f < right_n[0], lane_f + own_n, FAR)
-    right_far = jnp.where(right_n[1] > 0.0, lane_f - 80.0 + own_n + right_n[0], FAR)
-    right_pos = jnp.where(lane_f < 80.0, right_pos, jnp.where(lane_f < 96.0, right_far, FAR))
-    cot = (
-        dot(ones_where(t288 == own_pos).astype(BF16), own_cot)
-        + dot(ones_where(t288 == left_pos).astype(BF16), left_rows[...])
-        + dot(ones_where(t288 == right_pos).astype(BF16), right_rows[...])
-    )
-    grad2 = 0.5 * cot
-    grad2_low = grad2.astype(BF16)
-
     for step in range(4):
         for turn in range(4):
             theirs = block_of(
@@ -370,6 +423,26 @@
     slope_x = halves(slope_x * table_live)
     taps2 = halves(jnp.concatenate([dot(low_x, weights[4 + k]) for k in range(3)], axis=0))
 
+    arrive(left_rows.at[0:80], HALO)
+    arrive(right_rows.at[0:80], HALO + 1)
+    arrive(left_rows.at[80:96], HALO + 2)
+    arrive(right_rows.at[80:96], HALO + 3)
+    t288 = (iota((288, 1), 0) - 80).astype(F32)
+    own_pos = jnp.where(lane_f < own_n, lane_f, FAR)
+    left_pos = jnp.where(lane_f >= 80.0 - left_n[0], lane_f - 80.0, FAR)
+    left_far = jnp.where(left_n[1] > 0.0, lane_f - 96.0 - left_n[0], FAR)
+    left_pos = jnp.where(lane_f < 80.0, left_pos, jnp.where(lane_f < 96.0, left_far, FAR))
+    right_pos = jnp.where(lane_f < right_n[0], lane_f + own_n, FAR)
+    right_far = jnp.where(right_n[1] > 0.0, lane_f - 80.0 + own_n + right_n[0], FAR)
+    right_pos = jnp.where(lane_f < 80.0, right_pos, jnp.where(lane_f < 96.0, right_far, FAR))
+    cot = (
+        dot(ones_where(t288 == own_pos).astype(BF16), own_cot)
+        + dot(ones_where(t288 == left_pos).astype(BF16), left_rows[...])
+        + dot(ones_where(t288 == right_pos).astype(BF16), right_rows[...])
+    )
+    grad2 = 0.5 * cot
+    grad2_low = grad2.astype(BF16)
+
     hot2 = jnp.concatenate(
         [
             jnp.concatenate([hot_f[0:288], hot_f[64:352], hot_f[128:416]], axis=1),
@@ -464,16 +537,17 @@
     total = part_f32[two]
     for k in (1, 2, 3):
         total = total + recv1[(two + k) % 4].astype(F32)
-    part2[...] = total
+    part2_f32[...] = total
+    part2[...] = total.astype(SECOND_SUM)
     for k in (2, 1, 3):
         goal = (one + k) % 4
         push(part2.at[goal], recv2.at[one], R2 + one, chip(goal, two))
     for k in (1, 2, 3):
         source = (one + k) % 4
         arrive(recv2.at[source], R2 + source)
-    total = part2[one]
+    total = part2_f32[one]
     for k in (1, 2, 3):
-        total = total + recv2[(one + k) % 4]
+        total = total + recv2[(one + k) % 4].astype(F32)
     for k in range(16):
         part3[k] = total[k : k + 1]
     place = zl * 2 + zh
@@ -500,12 +574,23 @@
             jax.ShapeDtypeStruct((1, 4, CAP), F32),
             jax.ShapeDtypeStruct((1, 1152), F32),
         ),
-        in_specs=[vmem] * 11,
+        in_specs=[pl.BlockSpec(memory_space=pl.ANY)] * 11,
         out_specs=(vmem, vmem),
         scratch_shapes=[
-            pltpu.VMEM((32, B), F32),
-            pltpu.VMEM((32, B), BF16),
-            pltpu.VMEM((8, 32, B), BF16),
+            pltpu.VMEM((1, CAP), jnp.int32),
+            pltpu.SMEM((1, 1), jnp.int32),
+            pltpu.VMEM((1, CAP, C), BF16),
+            pltpu.VMEM((3, 6, B), BF16),
+            pltpu.VMEM((3, C), BF16),
+            pltpu.VMEM((3, 6, B), BF16),
+            pltpu.VMEM((3, C), BF16),
+            pltpu.VMEM((4, C), F32),
+            pltpu.VMEM((192, 192), BF16),
+            pltpu.VMEM((B, B), BF16),
+            pltpu.VMEM((128, 128), F32),
+            pltpu.VMEM((24, B), F32),
+            pltpu.VMEM((24, B), BF16),
+            pltpu.VMEM((8, 24, B), BF16),
             pltpu.VMEM((8, C, B), BF16),
             pltpu.VMEM((80, C), BF16),
             pltpu.VMEM((128, C), BF16),
@@ -520,12 +605,15 @@
             pltpu.VMEM((4, 4, 16, 1152), F32),
             pltpu.VMEM((4, 4, 16, 1152), FIRST_SUM),
             pltpu.VMEM((4, 4, 16, 1152), FIRST_SUM),
-            pltpu.VMEM((4, 16, 1152), F32),
+            pltpu.VMEM((4, 16, 1152), SECOND_SUM),
+            pltpu.VMEM((4, 16, 1152), SECOND_SUM),
             pltpu.VMEM((4, 16, 1152), F32),
             pltpu.VMEM((16, 1, 1152), F32),
             pltpu.VMEM((16, 1, 1152), F32),
             pltpu.SemaphoreType.DMA((80,)),
             pltpu.SemaphoreType.DMA((80,)),
+            pltpu.SemaphoreType.DMA((11,)),
+            pltpu.SemaphoreType.REGULAR((4,)),
         ],
         compiler_params=pltpu.CompilerParams(
             collective_id=0, has_side_effects=True, vmem_limit_bytes=60 * 1024 * 1024

time: 76.5 us -> 71 us (0.928)
  Pallas kernels: 72.3 us -> 67.3 us
    pallas_call x1, Pallas kernels: 72.3 us -> 67.3 us  [shards(): pl.pallas_call(kernel, out_shape=(jax.ShapeDtypeStruct((1, 4, CAP), F32),...]
where the time goes in v2:
time: 71 us; the launch traced here: 70.5 us
  Pallas kernels  67.3 us (95%)
  other arithmetic  1.31 us (2%)
  between operations  1.29 us (2%)
    pallas_call x1, Pallas kernels, shards(): pl.pallas_call(kernel, out_shape=(jax.ShapeDtypeStruct((1, 4, CAP), F32),...  67.3 us

profile of v2, /device:TPU:6, one launch (start us, length us, event | category | flops | bytes accessed | tf_op | source)
XLA Modules:
  0.0 70.5 jit_solution(18387148442323652851)
XLA Ops:
  1.3 67.3 %shard_map.122 = (f32[1,4,128]{2,1,0:T(4,128)}, f32[1,1152]{1,0:T(1,128)}) custom-call(s32[1,128]{1,0:T(1,128)} %bases_hbm.1, s32[1,1]{1,0:T(1,128)S(6)} %copy.14.len_hbm, bf16[1,128,768]{2,1,0:T(8,128)(2,1)} %cot_hbm.1, bf16[3,6,384]{2,1,0:T(8,128)(2,1)} %conv1_hbm.1, bf16[3,768]{1,0:T(4,128)(2,1)} %proj1_hbm.1, bf16[3,6,384]{2,1,0:T(8,128)(2,1)} %conv2_hbm.1, ...), custom_call_target="tpu_custom_call" | custom-call | tf_op jit(solution)/shard_map/pallas_call | solution.py:571
  68.6 0.0 copy-start
  68.6 1.3 %reduce = f32[1152]{0:T(1024)} reduce(f32[1,1152]{1,0:T(1,128)} %get-tuple-element.5, f32[]{:T(128)} %constant.16), dimensions={0}, to_apply=%get-tuple-element.5.reduce_sub_computation | reduce | bytes 9220 | tf_op jit(solution)/shard_map/pallas_call | solution.py:571
  70.0 0.0 copy-done
  70.0 0.6 copy.15
Async XLA Ops:
  68.6 1.3 %copy-start = (f32[1,4,128]{2,1,0:T(4,128)S(1)}, f32[1,4,128]{2,1,0:T(4,128)}, u32[]{:S(2)}) copy-start(f32[1,4,128]{2,1,0:T(4,128)} %get-tuple-element.8) | copy-start | bytes 6148

commit v3 on v2

--- a/solution.py
+++ b/solution.py
@@ -326,13 +326,12 @@
     push(line(1, 0, 0, 2), line(1, 0, 0, 2), D1H, one_up)
     to_second(1)
     to_sibling(1, 0)
+    heard(2)
+    announce(line_y, 3)
     arrive(line(2, 0), D1F + 1)
     push(line(2, 0, 2, 2), line(2, 0, 2, 2), D1H + 1, one_down)
     to_second(2)
     to_sibling(2, 0)
-    heard(2)
-    announce(line_y, 3)
-    relay_second(0)
     heard(3)
     for k in (1, 2, 3):
         push(enc_own, enc_all.at[k - 1], ENC + k - 1, along_seq(k))
@@ -341,6 +340,7 @@
     push(cot_ref.at[0, 0:80], right_rows.at[0:80], HALO + 1, along_seq(-1))
     push(tail.at[64:80], left_rows.at[80:96], HALO + 2, along_seq(2))
     push(cot_ref.at[0, 0:16], right_rows.at[80:96], HALO + 3, along_seq(-2))
+    relay_second(0)
     arrive(line(3, 0, 0, 2), D1H)
     arrive(line(3, 0, 2, 2), D1H + 1)
     to_second(3)
@@ -383,6 +383,26 @@
     hot_f = ones_where(triple_f == lane_f).astype(BF16)
     hot_r = ones_where(triple_r == lane_f).astype(BF16)
 
+    arrive(left_rows.at[0:80], HALO)
+    arrive(right_rows.at[0:80], HALO + 1)
+    arrive(left_rows.at[80:96], HALO + 2)
+    arrive(right_rows.at[80:96], HALO + 3)
+    t288 = (iota((288, 1), 0) - 80).astype(F32)
+    own_pos = jnp.where(lane_f < own_n, lane_f, FAR)
+    left_pos = jnp.where(lane_f >= 80.0 - left_n[0], lane_f - 80.0, FAR)
+    left_far = jnp.where(left_n[1] > 0.0, lane_f - 96.0 - left_n[0], FAR)
+    left_pos = jnp.where(lane_f < 80.0, left_pos, jnp.where(lane_f < 96.0, left_far, FAR))
+    right_pos = jnp.where(lane_f < right_n[0], lane_f + own_n, FAR)
+    right_far = jnp.where(right_n[1] > 0.0, lane_f - 80.0 + own_n + right_n[0], FAR)
+    right_pos = jnp.where(lane_f < 80.0, right_pos, jnp.where(lane_f < 96.0, right_far, FAR))
+    cot = (
+        dot(ones_where(t288 == own_pos).astype(BF16), own_cot)
+        + dot(ones_where(t288 == left_pos).astype(BF16), left_rows[...])
+        + dot(ones_where(t288 == right_pos).astype(BF16), right_rows[...])
+    )
+    grad2 = 0.5 * cot
+    grad2_low = grad2.astype(BF16)
+
     for step in range(4):
         for turn in range(4):
             theirs = block_of(
@@ -422,26 +442,6 @@
     low_x = (value_x * table_live).astype(BF16)
     slope_x = halves(slope_x * table_live)
     taps2 = halves(jnp.concatenate([dot(low_x, weights[4 + k]) for k in range(3)], axis=0))
-
-    arrive(left_rows.at[0:80], HALO)
-    arrive(right_rows.at[0:80], HALO + 1)
-    arrive(left_rows.at[80:96], HALO + 2)
-    arrive(right_rows.at[80:96], HALO + 3)
-    t288 = (iota((288, 1), 0) - 80).astype(F32)
-    own_pos = jnp.where(lane_f < own_n, lane_f, FAR)
-    left_pos = jnp.where(lane_f >= 80.0 - left_n[0], lane_f - 80.0, FAR)
-    left_far = jnp.where(left_n[1] > 0.0, lane_f - 96.0 - left_n[0], FAR)
-    left_pos = jnp.where(lane_f < 80.0, left_pos, jnp.where(lane_f < 96.0, left_far, FAR))
-    right_pos = jnp.where(lane_f < right_n[0], lane_f + own_n, FAR)
-    right_far = jnp.where(right_n[1] > 0.0, lane_f - 80.0 + own_n + right_n[0], FAR)
-    right_pos = jnp.where(lane_f < 80.0, right_pos, jnp.where(lane_f < 96.0, right_far, FAR))
-    cot = (
-        dot(ones_where(t288 == own_pos).astype(BF16), own_cot)
-        + dot(ones_where(t288 == left_pos).astype(BF16), left_rows[...])
-        + dot(ones_where(t288 == right_pos).astype(BF16), right_rows[...])
-    )
-    grad2 = 0.5 * cot
-    grad2_low = grad2.astype(BF16)
 
     hot2 = jnp.concatenate(
         [

time: 71 us -> 70.2 us (0.989)
    pallas_call x1, Pallas kernels: 67.3 us -> 66.6 us  [shards(): pl.pallas_call(kernel, out_shape=(jax.ShapeDtypeStruct((1, 4, CAP), F32),...]
where the time goes in v3:
time: 70.2 us; the launch traced here: 69.7 us
  Pallas kernels  66.6 us (95%)
  other arithmetic  1.31 us (2%)
  between operations  1.29 us (2%)
    pallas_call x1, Pallas kernels, shards(): pl.pallas_call(kernel, out_shape=(jax.ShapeDtypeStruct((1, 4, CAP), F32),...  66.6 us

profile of v3, /device:TPU:6, one launch (start us, length us, event | category | flops | bytes accessed | tf_op | source)
XLA Modules:
  0.0 69.7 jit_solution(10111626874770015693)
XLA Ops:
  1.3 66.6 %shard_map.122 = (f32[1,4,128]{2,1,0:T(4,128)}, f32[1,1152]{1,0:T(1,128)}) custom-call(s32[1,128]{1,0:T(1,128)} %bases_hbm.1, s32[1,1]{1,0:T(1,128)S(6)} %copy.14.len_hbm, bf16[1,128,768]{2,1,0:T(8,128)(2,1)} %cot_hbm.1, bf16[3,6,384]{2,1,0:T(8,128)(2,1)} %conv1_hbm.1, bf16[3,768]{1,0:T(4,128)(2,1)} %proj1_hbm.1, bf16[3,6,384]{2,1,0:T(8,128)(2,1)} %conv2_hbm.1, ...), custom_call_target="tpu_custom_call" | custom-call | tf_op jit(solution)/shard_map/pallas_call | solution.py:571
  67.8 0.0 copy-start
  67.9 1.3 %reduce = f32[1152]{0:T(1024)} reduce(f32[1,1152]{1,0:T(1,128)} %get-tuple-element.5, f32[]{:T(128)} %constant.16), dimensions={0}, to_apply=%get-tuple-element.5.reduce_sub_computation | reduce | bytes 9220 | tf_op jit(solution)/shard_map/pallas_call | solution.py:571
  69.2 0.0 copy-done
  69.2 0.6 copy.15
Async XLA Ops:
  67.8 1.3 %copy-start = (f32[1,4,128]{2,1,0:T(4,128)S(1)}, f32[1,4,128]{2,1,0:T(4,128)}, u32[]{:S(2)}) copy-start(f32[1,4,128]{2,1,0:T(4,128)} %get-tuple-element.8) | copy-start | bytes 6148

commit v4 on v3

--- a/solution.py
+++ b/solution.py
@@ -489,13 +489,6 @@
     mid1 = dot(own_hot, dot(mid1, classes).astype(BF16)).astype(BF16)
     sum1 = dot_tn(mid1, jnp.concatenate([grad1_low[16:144], grad1_low[176:304]], axis=0))
     to_core(0, sum1)
-    back1 = dot_nt(grad1_low, proj1)
-    gh1 = (back1 * pick(hot1, slope1)).astype(BF16)
-    near1 = [
-        jnp.concatenate([gh1[32:160], gh1[160:288]], axis=0),
-        jnp.concatenate([gh1[16:144], gh1[176:304]], axis=0),
-        jnp.concatenate([gh1[0:128], gh1[192:320]], axis=0),
-    ]
 
     for block in (1, 0):
         arrive(recv0.at[block], R0 + block)
@@ -510,6 +503,13 @@
         goal = (two + k) % 4
         push(part_low.at[goal], recv1.at[two], R1 + two, chip(one, goal))
 
+    back1 = dot_nt(grad1_low, proj1)
+    gh1 = (back1 * pick(hot1, slope1)).astype(BF16)
+    near1 = [
+        jnp.concatenate([gh1[32:160], gh1[160:288]], axis=0),
+        jnp.concatenate([gh1[16:144], gh1[176:304]], axis=0),
+        jnp.concatenate([gh1[0:128], gh1[192:320]], axis=0),
+    ]
     active1 = dot_nt(near1[0], weights[0])
     active1 = active1 + dot_nt(near1[1], weights[1])
     active1 = active1 + dot_nt(near1[2], weights[2])

time: 70.2 us -> 70.4 us (level)
  no operation moved by 1% of the time
where the time goes in v4:
time: 70.4 us; the launch traced here: 69.9 us
  Pallas kernels  66.7 us (95%)
  other arithmetic  1.31 us (2%)
  between operations  1.29 us (2%)
    pallas_call x1, Pallas kernels, shards(): pl.pallas_call(kernel, out_shape=(jax.ShapeDtypeStruct((1, 4, CAP), F32),...  66.7 us

profile of v4, /device:TPU:6, one launch (start us, length us, event | category | flops | bytes accessed | tf_op | source)
XLA Modules:
  0.0 69.9 jit_solution(13239014645649979382)
XLA Ops:
  1.3 66.7 %shard_map.122 = (f32[1,4,128]{2,1,0:T(4,128)}, f32[1,1152]{1,0:T(1,128)}) custom-call(s32[1,128]{1,0:T(1,128)} %bases_hbm.1, s32[1,1]{1,0:T(1,128)S(6)} %copy.14.len_hbm, bf16[1,128,768]{2,1,0:T(8,128)(2,1)} %cot_hbm.1, bf16[3,6,384]{2,1,0:T(8,128)(2,1)} %conv1_hbm.1, bf16[3,768]{1,0:T(4,128)(2,1)} %proj1_hbm.1, bf16[3,6,384]{2,1,0:T(8,128)(2,1)} %conv2_hbm.1, ...), custom_call_target="tpu_custom_call" | custom-call | tf_op jit(solution)/shard_map/pallas_call | solution.py:571
  68.0 0.0 copy-start
  68.0 1.3 %reduce = f32[1152]{0:T(1024)} reduce(f32[1,1152]{1,0:T(1,128)} %get-tuple-element.5, f32[]{:T(128)} %constant.16), dimensions={0}, to_apply=%get-tuple-element.5.reduce_sub_computation | reduce | bytes 9220 | tf_op jit(solution)/shard_map/pallas_call | solution.py:571
  69.3 0.0 copy-done
  69.3 0.6 copy.15
Async XLA Ops:
  68.0 1.3 %copy-start = (f32[1,4,128]{2,1,0:T(4,128)S(1)}, f32[1,4,128]{2,1,0:T(4,128)}, u32[]{:S(2)}) copy-start(f32[1,4,128]{2,1,0:T(4,128)} %get-tuple-element.8) | copy-start | bytes 6148
